TPU v7x, 128 devices: a whole 4x4x4 slice. The times are simulated.
128 devices in a mesh: scan: 16 (over z_lo, x, core), tgt: 8 (over y, z_hi).
Axes of the slice: x: 4, y: 4, z: 4 (z_hi: 2, z_lo: 2; z = z_hi * 2 + z_lo), core: 2. Of those that a mesh axis runs over, the one named last changes fastest.
Arguments:
- series: bfloat16 [96, 1200, 8192], P('scan', None, 'tgt'), as said below
- seed_index: int32 [512], replicated, may hold values from 0 to 8191
Outputs:
- affinity: bfloat16 [8192, 8192], P('tgt', 'scan')
Inputs may be any that keep to these rules, and one draw needn't show every extreme that they name: No grayordinate's series is constant over the frames of a scan.
All inputs are finite; a program needn't handle non-finite values.
Results may differ from a plain program's by a relative error of at most 0.0034.
Values may be sent and summed in bfloat16 or wider, within the bound.
A program may use at most 128 MiB of HBM per device.

v0:
```python
import jax
import jax.numpy as jnp
from jax import lax
from jax.sharding import PartitionSpec as P

epsilon = 1e-06
clip_level = 0.95


def fisher_map(values):
    clipped = jnp.clip(values, -clip_level, clip_level)
    return 0.5 * jnp.log((1.0 + clipped) / (1.0 - clipped))


def normalize_columns(profile):
    center = jnp.mean(profile, axis=0)
    deviate = profile - center
    spread = jnp.mean(deviate * deviate, axis=0)
    return (deviate * lax.rsqrt(spread + epsilon)).astype(jnp.bfloat16)


def body(series, seed_index):
    frame_count = series.shape[1]
    local_width = series.shape[2]
    seed_count = seed_index.shape[0]
    tgt_size = lax.axis_size("tgt")
    scan_size = lax.axis_size("scan")
    whole_width = local_width * tgt_size
    first_col = lax.axis_index("tgt") * local_width
    local_seed = seed_index - first_col
    inside = (local_seed >= 0) & (local_seed < local_width)
    safe_seed = jnp.clip(local_seed, 0, local_width - 1)
    values = series.astype(jnp.float32)
    center = jnp.mean(values, axis=1, keepdims=True)
    deviate = values - center
    spread = jnp.mean(deviate * deviate, axis=1, keepdims=True)
    standard = (deviate * lax.rsqrt(spread + epsilon)).astype(jnp.bfloat16)
    picked = jnp.take(standard, safe_seed, axis=2)
    picked = jnp.where(inside[None, None, :], picked, jnp.zeros_like(picked))
    seed_cols = lax.psum(picked, "tgt").astype(jnp.float32).astype(jnp.bfloat16)
    correl = (
        jnp.einsum("sfk,sfg->skg", seed_cols, standard, preferred_element_type=jnp.float32)
        / frame_count
    )
    running = jnp.sum(fisher_map(correl), axis=0)
    total = lax.psum(running, "scan")
    row_prof = normalize_columns(total)
    all_prof = lax.all_gather(row_prof, "tgt", axis=1, tiled=True)
    col_width = whole_width // scan_size
    col_prof = lax.dynamic_slice_in_dim(all_prof, lax.axis_index("scan") * col_width, col_width, 1)
    product = jnp.dot(row_prof.T, col_prof, preferred_element_type=jnp.float32)
    return jnp.tanh(product / seed_count).astype(jnp.bfloat16)


def solution(mesh):
    in_specs = (P("scan", None, "tgt"), P())
    out_specs = P("tgt", "scan")
    return jax.shard_map(body, mesh=mesh, in_specs=in_specs, out_specs=out_specs, check_vma=False)
```

profile of v0, /device:TPU:1, one launch (start us, length us, event | category | flops | bytes accessed | tf_op | source)
XLA Modules:
  0.0 716.5 jit_solution(13805646705477381361)
XLA Ops:
  6.5 0.0 all-reduce.3.cloned.1.call-start
  6.5 0.7 compare_and_fusion
  7.2 28.1 %copy.6 = bf16[6,1200,1024]{1,0,2:T(8,128)(2,1)} copy(bf16[6,1200,1024]{2,1,0:T(8,128)(2,1)} %param.2) | data formatting | bytes 29491200 | tf_op args[0]
  35.4 0.0 copy-start
  35.4 29.1 %convert_reduce_fusion = f32[6,1024]{0,1:T(8,128)S(1)} fusion(bf16[6,1200,1024]{1,0,2:T(8,128)(2,1)} %copy.6), kind=kLoop, calls=%fused_computation.2 | loop fusion | flops 14739456 | bytes 14770176 | tf_op jit(solution)/shard_map/reduce_sum | solution.py:34
  64.6 0.0 copy-done
  64.6 14.9 %fusion.2 = f32[6,1024]{0,1:T(8,128)S(1)} fusion(bf16[6,1200,1024]{1,0,2:T(8,128)(2,1)S(1)} %copy-done, f32[6,1024]{0,1:T(8,128)S(1)} %broadcast_multiply_fusion), kind=kLoop, calls=%fused_computation.5 | loop fusion | flops 29485056 | bytes 14794752 | tf_op jit(solution)/shard_map/reduce_sum | solution.py:36
  79.5 0.1 add_rsqrt_fusion
  79.6 10.1 %fusion.3 = bf16[6,1200,1024]{1,0,2:T(8,128)(2,1)} fusion(bf16[6,1200,1024]{1,0,2:T(8,128)(2,1)S(1)} %copy-done, f32[6,1024]{0,1:T(8,128)S(1)} %add_rsqrt_fusion, f32[6,1024]{0,1:T(8,128)S(1)} %broadcast_multiply_fusion), kind=kLoop, calls=%fused_computation.6 | loop fusion | flops 29491200 | bytes 29540352 | tf_op jit(solution)/shard_map/convert_element_type | solution.py:37
  89.7 21.0 %gather_fusion = bf16[512,6,1200]{2,1,0:T(8,128)(2,1)} fusion(bf16[6,1200,1024]{1,0,2:T(8,128)(2,1)} %fusion.3, s32[1024]{0:T(1024)S(1)} %pad_clamp_fusion), kind=kCustom, calls=%fused_computation | custom fusion | bytes 14747648 | tf_op jit(solution)/shard_map/jit(_take)/gather | solution.py:38
  110.7 14.7 %copy.7 = bf16[512,6,1200]{0,2,1:T(8,128)(2,1)} copy(bf16[512,6,1200]{2,1,0:T(8,128)(2,1)} %gather_fusion) | data formatting | bytes 14745600 | tf_op jit(solution)/shard_map/jit(_take)/gather | solution.py:38
  125.3 6.9 select_bitcast_fusion
  132.3 0.0 all-reduce.3.cloned.1.call-update
  132.3 0.2 all-reduce.5.cloned.1.call-start
  132.5 308.2 %all-reduce.3.cloned.1.call-done = bf16[6,1200,512]{2,1,0:T(8,128)(2,1)} async-done(((bf16[6,1200,512]{2,1,0:T(8,128)(2,1)}), bf16[6,1200,512]{2,1,0:T(8,128)(2,1)}) %all-reduce.3.cloned.1.call-update) | async-done | bytes 7372816 | tf_op jit(solution)/shard_map/psum | solution.py:40
  440.7 22.3 %multiply_reduce_fusion = f32[512,1024]{1,0:T(8,128)} fusion(bf16[6,1200,512]{2,1,0:T(8,128)(2,1)} %all-reduce.3.cloned.1.call-done, bf16[6,1200,1024]{1,0,2:T(8,128)(2,1)} %fusion.3), kind=kOutput, calls=%fused_computation.9 | convolution fusion | flops 7571243008 | bytes 24215552 | tf_op jit(solution)/shard_map/sfk,sfg->skg/dot_general | solution.py:42
  463.1 0.0 all-reduce.5.cloned.1.call-update
  463.1 0.0 all-gather.2.cloned.1.call-start
  463.1 127.2 %all-reduce.5.cloned.1.call-done = f32[512,1024]{1,0:T(8,128)} async-done(((f32[512,1024]{1,0:T(8,128)}), f32[512,1024]{1,0:T(8,128)}) %all-reduce.5.cloned.1.call-update) | async-done | bytes 2097168 | tf_op jit(solution)/shard_map/psum | solution.py:46
  590.3 1.7 reduce_sum.48
  592.0 1.8 multiply_reduce_fusion.1
  593.9 2.9 multiply_convert_fusion
  596.8 0.0 all-gather.2.cloned.1.call-update
  596.9 109.9 %all-gather.2.cloned.1.call-done = bf16[512,8192]{1,0:T(8,128)(2,1)} async-done(((bf16[512,1024]{1,0:T(8,128)(2,1)}), bf16[512,8192]{1,0:T(8,128)(2,1)}) %all-gather.2.cloned.1.call-update) | async-done | bytes 8388624 | tf_op jit(solution)/shard_map/all_gather | solution.py:48
  706.8 3.1 tanh_convert_fusion
  (4 shorter events, 0.1 us)
Async XLA Ops:
  6.5 434.2 %all-reduce.3.cloned.1.call-start = ((), (), s32[]{:S(2)}) async-start(), calls=%async_computation | async-start | bytes 14745600 | tf_op jit(solution)/shard_map/psum | solution.py:40
  35.4 29.2 %copy-start = (bf16[6,1200,1024]{1,0,2:T(8,128)(2,1)S(1)}, bf16[6,1200,1024]{1,0,2:T(8,128)(2,1)}, u32[]{:S(2)}) copy-start(bf16[6,1200,1024]{1,0,2:T(8,128)(2,1)} %copy.6) | copy-start | bytes 44236804
  132.3 458.0 %all-reduce.5.cloned.1.call-start = ((), (), s32[]{:S(2)}) async-start(), calls=%async_computation.1 | async-start | bytes 4194304 | tf_op jit(solution)/shard_map/psum | solution.py:46
  463.1 243.7 %all-gather.2.cloned.1.call-start = ((), (), s32[]{:S(2)}) async-start(), calls=%async_computation.2 | async-start | bytes 9437184 | tf_op jit(solution)/shard_map/all_gather | solution.py:48
Sparse Core Ops, SparseCore 0:
  132.4 308.2 all-reduce.2
  463.2 127.0 all-reduce.4
  597.0 109.7 all-gather.1
where the time goes:
time: 718 us; the launch traced here: 716 us
  waiting for transfers between devices  545 us (76%)
  other arithmetic  68.4 us (10%)
  local copies, waits for them, and re-layouts  63.8 us (9%)
  matrix products  25.4 us (4%)
  between operations  13.2 us (2%)
    psum x1, waiting for transfers between devices, body(): seed_cols = lax.psum(picked, 'tgt').astype(jnp.float32).astype(jnp.bfloat16)  308 us
    psum x1, waiting for transfers between devices, body(): total = lax.psum(running, 'scan')  127 us
    all_gather x1, waiting for transfers between devices, body(): all_prof = lax.all_gather(row_prof, 'tgt', axis=1, tiled=True)  110 us
    gather x2, local copies, waits for them, and re-layouts, body(): picked = jnp.take(standard, safe_seed, axis=2)  35.6 us
    reduce_sum x1, other arithmetic, body(): center = jnp.mean(values, axis=1, keepdims=True)  29.1 us
    unnamed x3, local copies, waits for them, and re-layouts  28.2 us
    dot_general x1, matrix products, body(): jnp.einsum('sfk,sfg->skg', seed_cols, standard, preferred_element_type=jn...  22.3 us
    reduce_sum x1, other arithmetic, body(): spread = jnp.mean(deviate * deviate, axis=1, keepdims=True)  14.9 us
  transfers between devices with their start and end apart: 3, of which 3 were waited for; matrix products, arithmetic and copies ran while one was open for 0% of the time, Pallas kernels for 0%

commit v1 on v0

--- a/solution.py
+++ b/solution.py
@@ -43,7 +43,7 @@
         / frame_count
     )
     running = jnp.sum(fisher_map(correl), axis=0)
-    total = lax.psum(running, "scan")
+    total = jnp.sum(lax.all_gather(running, "scan"), axis=0)
     row_prof = normalize_columns(total)
     all_prof = lax.all_gather(row_prof, "tgt", axis=1, tiled=True)
     col_width = whole_width // scan_size

time: 718 us -> 787 us (1.096)
  waiting for transfers between devices: 545 us -> 593 us
  other arithmetic: 68.4 us -> 90.7 us
    all_gather x0 -> x1, waiting for transfers between devices: none -> 176 us  [body(): total = jnp.sum(lax.all_gather(running, 'scan'), axis=0)]
    psum x1 -> x0, waiting for transfers between devices: 127 us -> none  [body(): total = lax.psum(running, 'scan')]
    reduce_sum x1, other arithmetic: 1.74 us -> 15 us  [normalize_columns(): center = jnp.mean(profile, axis=0)]
    reduce_sum x0 -> x1, other arithmetic: none -> 12.1 us  [body(): total = jnp.sum(lax.all_gather(running, 'scan'), axis=0)]
where the time goes in v1:
time: 787 us; the launch traced here: 786 us
  waiting for transfers between devices  593 us (75%)
  other arithmetic  90.7 us (12%)
  local copies, waits for them, and re-layouts  63.8 us (8%)
  matrix products  25.3 us (3%)
  between operations  13.2 us (2%)
    psum x1, waiting for transfers between devices, body(): seed_cols = lax.psum(picked, 'tgt').astype(jnp.float32).astype(jnp.bfloat16)  308 us
    all_gather x1, waiting for transfers between devices, body(): total = jnp.sum(lax.all_gather(running, 'scan'), axis=0)  176 us
    all_gather x1, waiting for transfers between devices, body(): all_prof = lax.all_gather(row_prof, 'tgt', axis=1, tiled=True)  109 us
    gather x2, local copies, waits for them, and re-layouts, body(): picked = jnp.take(standard, safe_seed, axis=2)  35.6 us
    reduce_sum x1, other arithmetic, body(): center = jnp.mean(values, axis=1, keepdims=True)  29.1 us
    unnamed x3, local copies, waits for them, and re-layouts  28.2 us
    dot_general x1, matrix products, body(): jnp.einsum('sfk,sfg->skg', seed_cols, standard, preferred_element_type=jn...  22.2 us
  transfers between devices with their start and end apart: 3, of which 3 were waited for; matrix products, arithmetic and copies ran while one was open for 0% of the time, Pallas kernels for 0%

profile of v1, /device:TPU:1, one launch (start us, length us, event | category | flops | bytes accessed | tf_op | source)
XLA Modules:
  0.0 786.0 jit_solution(1042595827996808843)
XLA Ops:
  6.5 0.0 all-reduce.2.cloned.1.call-start
  6.5 0.7 compare_and_fusion
  7.2 28.1 %copy.6 = bf16[6,1200,1024]{1,0,2:T(8,128)(2,1)} copy(bf16[6,1200,1024]{2,1,0:T(8,128)(2,1)} %param.2) | data formatting | bytes 29491200 | tf_op args[0]
  35.4 0.0 copy-start
  35.4 29.1 %convert_reduce_fusion = f32[6,1024]{0,1:T(8,128)S(1)} fusion(bf16[6,1200,1024]{1,0,2:T(8,128)(2,1)} %copy.6), kind=kLoop, calls=%fused_computation.2 | loop fusion | flops 14739456 | bytes 14770176 | tf_op jit(solution)/shard_map/reduce_sum | solution.py:34
  64.6 0.0 copy-done
  64.6 14.9 %fusion.2 = f32[6,1024]{0,1:T(8,128)S(1)} fusion(bf16[6,1200,1024]{1,0,2:T(8,128)(2,1)S(1)} %copy-done, f32[6,1024]{0,1:T(8,128)S(1)} %broadcast_multiply_fusion), kind=kLoop, calls=%fused_computation.5 | loop fusion | flops 29485056 | bytes 14794752 | tf_op jit(solution)/shard_map/reduce_sum | solution.py:36
  79.5 0.1 add_rsqrt_fusion
  79.6 10.1 %fusion.3 = bf16[6,1200,1024]{1,0,2:T(8,128)(2,1)} fusion(bf16[6,1200,1024]{1,0,2:T(8,128)(2,1)S(1)} %copy-done, f32[6,1024]{0,1:T(8,128)S(1)} %add_rsqrt_fusion, f32[6,1024]{0,1:T(8,128)S(1)} %broadcast_multiply_fusion), kind=kLoop, calls=%fused_computation.6 | loop fusion | flops 29491200 | bytes 29540352 | tf_op jit(solution)/shard_map/convert_element_type | solution.py:37
  89.7 21.0 %gather_fusion = bf16[512,6,1200]{2,1,0:T(8,128)(2,1)} fusion(bf16[6,1200,1024]{1,0,2:T(8,128)(2,1)} %fusion.3, s32[1024]{0:T(1024)S(1)} %pad_clamp_fusion), kind=kCustom, calls=%fused_computation | custom fusion | bytes 14747648 | tf_op jit(solution)/shard_map/jit(_take)/gather | solution.py:38
  110.7 14.7 %copy.7 = bf16[512,6,1200]{0,2,1:T(8,128)(2,1)} copy(bf16[512,6,1200]{2,1,0:T(8,128)(2,1)} %gather_fusion) | data formatting | bytes 14745600 | tf_op jit(solution)/shard_map/jit(_take)/gather | solution.py:38
  125.3 6.9 select_bitcast_fusion
  132.3 0.0 all-reduce.2.cloned.1.call-update
  132.3 0.2 all-gather.6.cloned.1.call-start
  132.5 308.2 %all-reduce.2.cloned.1.call-done = bf16[6,1200,512]{2,1,0:T(8,128)(2,1)} async-done(((bf16[6,1200,512]{2,1,0:T(8,128)(2,1)}), bf16[6,1200,512]{2,1,0:T(8,128)(2,1)}) %all-reduce.2.cloned.1.call-update) | async-done | bytes 7372816 | tf_op jit(solution)/shard_map/psum | solution.py:40
  440.7 22.2 %multiply_reduce_fusion = f32[512,1024]{1,0:T(8,128)} fusion(bf16[6,1200,512]{2,1,0:T(8,128)(2,1)} %all-reduce.2.cloned.1.call-done, bf16[6,1200,1024]{1,0,2:T(8,128)(2,1)} %fusion.3), kind=kOutput, calls=%fused_computation.9 | convolution fusion | flops 7571243008 | bytes 24215552 | tf_op jit(solution)/shard_map/sfk,sfg->skg/dot_general | solution.py:42
  463.0 0.0 all-gather.6.cloned.1.call-update
  463.0 0.0 all-gather.4.cloned.1.call-start
  463.0 175.5 %all-gather.6.cloned.1.call-done = f32[8192,1024]{1,0:T(8,128)} async-done(((f32[512,1024]{1,0:T(8,128)}), f32[8192,1024]{1,0:T(8,128)}) %all-gather.6.cloned.1.call-update) | async-done | bytes 33554448 | tf_op jit(solution)/shard_map/all_gather | solution.py:46
  638.6 12.1 %reduce_sum.57 = f32[512,1024]{1,0:T(8,128)S(1)} reduce(f32[16,512,1024]{2,1,0:T(8,128)} %bitcast.5, f32[]{:T(128)} %constant.23.clone.1), dimensions={0}, to_apply=%region_4.5 | reduce | flops 7864320 | bytes 35651588 | tf_op jit(solution)/shard_map/reduce_sum | solution.py:46
  650.7 15.0 %reduce_sum.58 = f32[1024]{0:T(1024)S(1)} reduce(f32[8192,1024]{1,0:T(8,128)} %all-gather.6.cloned.1.call-done, f32[]{:T(128)} %constant.23.clone.1), dimensions={0}, to_apply=%region_5.6 | reduce | flops 8387584 | bytes 33558532 | tf_op jit(solution)/shard_map/reduce_sum | solution.py:16
  665.7 0.3 multiply_reduce_fusion.1
  666.0 1.4 multiply_convert_fusion
  667.3 0.0 all-gather.4.cloned.1.call-update
  667.4 109.0 %all-gather.4.cloned.1.call-done = bf16[512,8192]{1,0:T(8,128)(2,1)} async-done(((bf16[512,1024]{1,0:T(8,128)(2,1)}), bf16[512,8192]{1,0:T(8,128)(2,1)}) %all-gather.4.cloned.1.call-update) | async-done | bytes 8388624 | tf_op jit(solution)/shard_map/all_gather | solution.py:48
  776.3 3.1 tanh_convert_fusion
  (4 shorter events, 0.1 us)
Async XLA Ops:
  6.5 434.2 %all-reduce.2.cloned.1.call-start = ((), (), s32[]{:S(2)}) async-start(), calls=%async_computation | async-start | bytes 14745600 | tf_op jit(solution)/shard_map/psum | solution.py:40
  35.4 29.2 %copy-start = (bf16[6,1200,1024]{1,0,2:T(8,128)(2,1)S(1)}, bf16[6,1200,1024]{1,0,2:T(8,128)(2,1)}, u32[]{:S(2)}) copy-start(bf16[6,1200,1024]{1,0,2:T(8,128)(2,1)} %copy.6) | copy-start | bytes 44236804
  132.3 506.3 %all-gather.6.cloned.1.call-start = ((), (), s32[]{:S(2)}) async-start(), calls=%async_computation.2 | async-start | bytes 35651584 | tf_op jit(solution)/shard_map/all_gather | solution.py:46
  463.0 313.3 %all-gather.4.cloned.1.call-start = ((), (), s32[]{:S(2)}) async-start(), calls=%async_computation.1 | async-start | bytes 9437184 | tf_op jit(solution)/shard_map/all_gather | solution.py:48
Sparse Core Ops, SparseCore 0:
  132.4 308.2 all-reduce.1
  463.1 175.4 all-gather.5
  667.5 108.7 all-gather.3
